TPU v7x, 256 devices: a whole 4x4x8 slice. The times are simulated.
256 devices in a mesh: tp: 8 (over y, core), ep: 32 (over z, x).
Axes of the slice: x: 4, y: 4, z: 8, core: 2. Of those that a mesh axis runs over, the one named last changes fastest.
Arguments:
- tokens: bfloat16 [512, 8192], P('ep'), may hold values from -6 to 6
- cotangent: bfloat16 [512, 8192], P('ep'), may hold values from -6 to 6
- w_gate: bfloat16 [14336, 8192], P(('tp', 'ep')), may hold values from -0.0625 to 0.0625
- w_up: bfloat16 [14336, 8192], P(('tp', 'ep')), may hold values from -0.0625 to 0.0625
- w_down: bfloat16 [14336, 8192], P(('tp', 'ep')), may hold values from -0.375 to 0.375
- neuron_expert: int32 [14336], P(('tp', 'ep')), may hold values from 0 to 63, as said below
- neuron_slot: int32 [14336], P(('tp', 'ep')), may hold values from 0 to 63, as said below
- choice_expert: int32 [512, 8], P('ep'), may hold values from 0 to 63, all different within a row; in each aligned block of 16 rows (0 to 15, 16 to 31, ...) at most 4 rows name the same one
- choice_weight: float32 [512, 8], P('ep'), may hold values from 0.02 to 0.3
Outputs:
- output: bfloat16 [512, 8192], P('ep', 'tp')
- d_tokens: bfloat16 [512, 8192], P('ep', 'tp')
- d_weight: float32 [512, 8], P('ep')
- d_gate_exp: bfloat16 [64, 512, 8192], P('ep', 'tp')
- d_up_exp: bfloat16 [64, 512, 8192], P('ep', 'tp')
- d_down_exp: bfloat16 [64, 512, 8192], P('ep', 'tp')
Inputs may be any that keep to these rules, and one draw needn't show every extreme that they name: `neuron_expert`: expert e belongs to ep index e // 2. Among the 56 neurons starting at any multiple of 56, at most 4 name experts of one ep index. `neuron_slot`: within each tp range of 1792 neurons, the neurons of one expert have distinct slots. `choice_expert`: each row names 8 different experts; in each aligned block of 16 rows no expert is named more than 4 times.
All inputs are finite; a program needn't handle non-finite values.
Results may differ from a plain program's by a relative error of at most 0.018.
Values may be sent and summed in bfloat16 or wider, within the bound.
No kernel may reach another device: no remote copies, remote signals or barrier semaphores. Data moves between devices by JAX's collectives and lax.ppermute only.
A program may use at most 128 MiB of HBM per device.

v0:
```python
import jax
import jax.numpy as jnp
from jax import lax
from jax.sharding import PartitionSpec as P

NL = 56
E_DEV = 2
TOPK = 8


def earlier_same(labels):
    count = labels.shape[0]
    row_iota = lax.broadcasted_iota(jnp.int32, (count, count), 0)
    col_iota = lax.broadcasted_iota(jnp.int32, (count, count), 1)
    same = (labels[:, None] == labels[None, :]) & (col_iota < row_iota)
    return jnp.sum(same.astype(jnp.int32), 1)


def slope_of(gate):
    sig = jax.nn.sigmoid(gate)
    return sig * (1.0 + gate * (1.0 - sig))


def source_table(matches):
    column = lax.broadcasted_iota(jnp.int32, matches.shape, 1)
    index = jnp.sum(jnp.where(matches, column, 0), 1)
    return (index, jnp.any(matches, 1))


def pick_rows(rows, index, filled):
    taken = jnp.take(rows, index, axis=0)
    return jnp.where(filled[:, None], taken, jnp.zeros_like(taken))


def dispatch(rows):
    return lax.all_to_all(rows, "ep", split_axis=0, concat_axis=0, tiled=True)


def to_sources(terms, n_ep, tcap):
    shares = []
    for term in terms:
        share = lax.psum_scatter(term.astype(jnp.bfloat16), "tp", scatter_dimension=1, tiled=True)
        shares.append(share.reshape(n_ep, tcap, -1))
    stacked = jnp.stack(shares, 1).reshape(n_ep, E_DEV * tcap, -1)
    moved = lax.all_to_all(stacked, "ep", split_axis=0, concat_axis=0, tiled=True)
    return moved.reshape(-1, stacked.shape[2])


def body(
    tokens,
    cotangent,
    w_gate,
    w_up,
    w_down,
    neuron_expert,
    neuron_slot,
    choice_expert,
    choice_weight,
):
    n_ep = lax.axis_size("ep")
    n_tp = lax.axis_size("tp")
    width = tokens.shape[1]
    local_width = width // n_tp
    peer_slots = 2 * ((NL + n_ep - 1) // n_ep)
    capacity = n_ep * peer_slots // E_DEV
    owner = neuron_expert // E_DEV
    target = owner * peer_slots + earlier_same(owner)
    packing = target[None, :] == jnp.arange(n_ep * peer_slots, dtype=jnp.int32)[:, None]
    pack_index, pack_filled = source_table(packing)
    labels = neuron_expert % E_DEV * capacity + neuron_slot + 1
    packed_labels = jnp.sum(jnp.where(packing, labels[None, :], 0), 1)
    packed_labels = packed_labels.astype(jnp.float32).astype(jnp.bfloat16).reshape(n_ep, peer_slots)

    def pack(weight):
        return pick_rows(weight, pack_index, pack_filled).reshape(n_ep, peer_slots, width)

    got_gate, got_up, got_down, got_labels = (
        lax.all_to_all(pack(w_gate), "ep", split_axis=0, concat_axis=0, tiled=True),
        lax.all_to_all(pack(w_up), "ep", split_axis=0, concat_axis=0, tiled=True),
        lax.all_to_all(pack(w_down), "ep", split_axis=0, concat_axis=0, tiled=True),
        lax.all_to_all(packed_labels, "ep", split_axis=0, concat_axis=0, tiled=True),
    )
    slot_of = got_labels.reshape(-1).astype(jnp.int32) - 1
    placing = slot_of[None, :] == jnp.arange(E_DEV * capacity, dtype=jnp.int32)[:, None]
    place_index, place_filled = source_table(placing)

    def place(rows):
        return pick_rows(rows.reshape(-1, width), place_index, place_filled).reshape(
            E_DEV, capacity, width
        )

    gate_exp = place(got_gate)
    up_exp = place(got_up)
    down_exp = place(got_down)
    tok_dev = tokens.shape[0]
    chosen = choice_expert.reshape(-1)
    count = chosen.shape[0]
    experts_all = E_DEV * n_ep
    tcap = max(2, 2 * count // experts_all)
    slot_ids = chosen * tcap + earlier_same(chosen)
    matching = slot_ids[None, :] == jnp.arange(experts_all * tcap, dtype=jnp.int32)[:, None]
    choice_of_slot, slot_used = source_table(matching)
    send_x = pick_rows(tokens, choice_of_slot // TOPK, slot_used)
    send_x = send_x.reshape(n_ep, E_DEV * tcap, width)
    x_got = dispatch(send_x).reshape(n_ep, E_DEV, tcap, width)
    saved = []
    terms = []
    for local in range(E_DEV):
        x_rows = x_got[:, local].reshape(-1, width)
        gate = jnp.einsum("rd,hd->rh", x_rows, gate_exp[local], preferred_element_type=jnp.float32)
        upper = jnp.einsum("rd,hd->rh", x_rows, up_exp[local], preferred_element_type=jnp.float32)
        hidden = (jax.nn.silu(gate) * upper).astype(jnp.bfloat16)
        terms.append(jnp.dot(hidden, down_exp[local], preferred_element_type=jnp.float32))
        saved.append((x_rows, gate, upper, hidden))
    results = to_sources(terms, n_ep, tcap)
    per_choice = jnp.take(results, slot_ids, axis=0).astype(jnp.float32)
    weights = choice_weight.reshape(-1, 1)
    output = jnp.sum((weights * per_choice).reshape(tok_dev, TOPK, local_width), 1).astype(
        jnp.bfloat16
    )
    cot_local = lax.dynamic_slice_in_dim(
        cotangent, lax.axis_index("tp") * local_width, local_width, 1
    ).astype(jnp.float32)
    partial_value = jnp.sum(
        per_choice.reshape(tok_dev, TOPK, local_width) * cot_local[:, None, :], 2
    )
    d_weight = lax.psum(partial_value, "tp")
    slot_weight = jnp.take(choice_weight.reshape(-1), choice_of_slot, axis=0)
    slot_cot = jnp.take(cotangent, choice_of_slot // TOPK, axis=0).astype(jnp.float32)
    scaled_rows = (slot_weight[:, None] * slot_cot).astype(jnp.bfloat16)
    send_g = jnp.where(slot_used[:, None], scaled_rows, jnp.zeros_like(scaled_rows))
    send_g = send_g.reshape(n_ep, E_DEV * tcap, width)
    g_got = dispatch(send_g).reshape(n_ep, E_DEV, tcap, width)
    grad_gate = []
    grad_up = []
    grad_down = []
    back_terms = []
    for local in range(E_DEV):
        x_rows, gate, upper, hidden = saved[local]
        g_rows = g_got[:, local].reshape(-1, width)
        d_hidden = jnp.einsum(
            "rd,hd->rh", g_rows, down_exp[local], preferred_element_type=jnp.float32
        )
        grad_down.append(
            jnp.einsum("rh,rd->hd", hidden, g_rows, preferred_element_type=jnp.float32).astype(
                jnp.bfloat16
            )
        )
        d_gate_rows = (d_hidden * upper * slope_of(gate)).astype(jnp.bfloat16)
        d_up_rows = (d_hidden * jax.nn.silu(gate)).astype(jnp.bfloat16)
        grad_gate.append(
            jnp.einsum("rh,rd->hd", d_gate_rows, x_rows, preferred_element_type=jnp.float32).astype(
                jnp.bfloat16
            )
        )
        grad_up.append(
            jnp.einsum("rh,rd->hd", d_up_rows, x_rows, preferred_element_type=jnp.float32).astype(
                jnp.bfloat16
            )
        )
        term = jnp.dot(d_gate_rows, gate_exp[local], preferred_element_type=jnp.float32)
        term = term + jnp.dot(d_up_rows, up_exp[local], preferred_element_type=jnp.float32)
        back_terms.append(term)
    d_rows = to_sources(back_terms, n_ep, tcap)
    d_choice = jnp.take(d_rows, slot_ids, axis=0).astype(jnp.float32)
    d_tokens = jnp.sum(d_choice.reshape(tok_dev, TOPK, local_width), 1).astype(jnp.bfloat16)
    return (
        output,
        d_tokens,
        d_weight,
        jnp.stack(grad_gate, 0),
        jnp.stack(grad_up, 0),
        jnp.stack(grad_down, 0),
    )


def solution(mesh):
    in_specs = (
        P("ep", None),
        P("ep", None),
        P(("tp", "ep"), None),
        P(("tp", "ep"), None),
        P(("tp", "ep"), None),
        P(("tp", "ep")),
        P(("tp", "ep")),
        P("ep", None),
        P("ep", None),
    )
    out_specs = (
        P("ep", "tp"),
        P("ep", "tp"),
        P("ep", None),
        P("ep", "tp", None),
        P("ep", "tp", None),
        P("ep", "tp", None),
    )
    return jax.shard_map(body, mesh=mesh, in_specs=in_specs, out_specs=out_specs, check_vma=False)
```

profile of v0, /device:TPU:2, one launch (start us, length us, event | category | flops | bytes accessed | tf_op | source)
XLA Modules:
  0.0 628.7 jit_solution(13298264075085638580)
XLA Ops:
  9.0 11.6 %all-to-all-start.1 = ((bf16[32,1,4]{2,1,0:T(2,128)(2,1)}), bf16[32,1,4]{2,1,0:T(2,128)(2,1)S(1)}, u32[]{:S(2)}, u32[]{:S(2)}) async-start(bf16[32,1,4]{2,1,0:T(2,128)(2,1)} %convert_element_type.135), calls=%async_computation.1 | async-start | bytes 32768 | tf_op jit(solution)/shard_map/all_to_all | solution.py:81
  20.8 3.2 gather_fusion.6
  30.3 5.6 select_select_fusion.2
  35.9 4.1 reshape.188
  40.0 9.8 %all-to-all-start.4 = ((bf16[32,4,8192]{2,1,0:T(4,128)(2,1)}), bf16[32,4,8192]{2,1,0:T(4,128)(2,1)}, u32[]{:S(2)}, u32[]{:S(2)}) async-start(bf16[32,4,8192]{2,1,0:T(4,128)(2,1)} %reshape.188), calls=%async_computation.4 | async-start | bytes 4194304 | tf_op jit(solution)/shard_map/all_to_all | solution.py:80
  49.9 4.1 reshape.186
  54.0 44.7 %all-to-all-done.4 = bf16[32,4,8192]{2,1,0:T(4,128)(2,1)} async-done(((bf16[32,4,8192]{2,1,0:T(4,128)(2,1)}), bf16[32,4,8192]{2,1,0:T(4,128)(2,1)}, u32[]{:S(2)}, u32[]{:S(2)}) %all-to-all-start.4) | async-done | bytes 2097184 | tf_op jit(solution)/shard_map/all_to_all | solution.py:80
  98.7 6.8 %all-to-all-start.3 = ((bf16[32,4,8192]{2,1,0:T(4,128)(2,1)}), bf16[32,4,8192]{2,1,0:T(4,128)(2,1)}, u32[]{:S(2)}, u32[]{:S(2)}) async-start(bf16[32,4,8192]{2,1,0:T(4,128)(2,1)} %reshape.186), calls=%async_computation.3 | async-start | bytes 4194304 | tf_op jit(solution)/shard_map/all_to_all | solution.py:79
  107.7 47.0 %all-to-all-done.3 = bf16[32,4,8192]{2,1,0:T(4,128)(2,1)} async-done(((bf16[32,4,8192]{2,1,0:T(4,128)(2,1)}), bf16[32,4,8192]{2,1,0:T(4,128)(2,1)}, u32[]{:S(2)}, u32[]{:S(2)}) %all-to-all-start.3) | async-done | bytes 2097184 | tf_op jit(solution)/shard_map/all_to_all | solution.py:79
  154.7 5.6 all-to-all-start.2
  161.0 5.2 gather_fusion.9
  166.2 5.1 gather_fusion.1
  173.3 6.2 fusion.9
  179.5 28.3 %all-to-all-done.2 = bf16[32,4,8192]{2,1,0:T(4,128)(2,1)S(1)} async-done(((bf16[32,4,8192]{2,1,0:T(4,128)(2,1)}), bf16[32,4,8192]{2,1,0:T(4,128)(2,1)S(1)}, u32[]{:S(2)}, u32[]{:S(2)}) %all-to-all-start.2) | async-done | bytes 2097184 | tf_op jit(solution)/shard_map/all_to_all | solution.py:78
  207.7 99.2 %all_to_all.41 = bf16[32,8,8192]{2,1,0:T(8,128)(2,1)} all-to-all(bf16[32,8,8192]{2,1,0:T(8,128)(2,1)} %get-tuple-element.51), channel_id=1, replica_groups=mesh['tp'=8,'ep'=32] {'ep'}, dimensions={0} | all-to-all | bytes 8388608 | tf_op jit(solution)/shard_map/all_to_all | solution.py:36
  306.9 5.6 all-to-all-start.6
  330.4 5.9 select_select_fusion.1
  336.3 7.2 %reshape.183 = bf16[32,2,4,8192]{3,2,1,0:T(4,128)(2,1)} reshape(bf16[32,8,8192]{2,1,0:T(8,128)(2,1)} %all_to_all.41) | data formatting | bytes 8388608 | tf_op jit(solution)/shard_map/reshape | solution.py:105
  343.5 5.4 fusion.45
  355.2 49.9 %all-to-all-done.6 = bf16[32,8,8192]{2,1,0:T(8,128)(2,1)} async-done(((bf16[32,8,8192]{2,1,0:T(8,128)(2,1)}), bf16[32,8,8192]{2,1,0:T(8,128)(2,1)}, u32[]{:S(2)}, u32[]{:S(2)}) %all-to-all-start.6) | async-done | bytes 4194336 | tf_op jit(solution)/shard_map/all_to_all | solution.py:36
  405.1 7.2 %reshape.194 = bf16[32,2,4,8192]{3,2,1,0:T(4,128)(2,1)} reshape(bf16[32,8,8192]{2,1,0:T(8,128)(2,1)} %all-to-all-done.6) | data formatting | bytes 8388608 | tf_op jit(solution)/shard_map/reshape | solution.py:133
  412.3 5.4 fusion.44
  417.7 4.1 reshape_squeeze.15
  429.0 3.9 reshape_squeeze.14
  461.0 37.3 %reduce-scatter.5.cloned.1.call-done = bf16[128,1024]{1,0:T(8,128)(2,1)} async-done(((bf16[128,8192]{1,0:T(8,128)(2,1)}), bf16[128,1024]{1,0:T(8,128)(2,1)}) %reduce-scatter.5.cloned.1.call-update) | async-done | bytes 262160 | tf_op jit(solution)/shard_map/reduce_scatter | solution.py:42
  500.7 10.1 %all-to-all-start.5 = ((bf16[32,8,1024]{2,1,0:T(8,128)(2,1)}), bf16[32,8,1024]{2,1,0:T(8,128)(2,1)S(1)}, u32[]{:S(2)}, u32[]{:S(2)}) async-start(bf16[32,8,1024]{2,1,0:T(8,128)(2,1)} %copy.42), calls=%async_computation.7 | async-start | bytes 1048576 | tf_op jit(solution)/shard_map/all_to_all | solution.py:45
  510.8 3.2 pad_maximum_fusion.2
  514.0 23.2 %reduce-scatter.11.cloned.1.call-done = bf16[128,1024]{1,0:T(8,128)(2,1)} async-done(((bf16[128,8192]{1,0:T(8,128)(2,1)}), bf16[128,1024]{1,0:T(8,128)(2,1)}) %reduce-scatter.11.cloned.1.call-update) | async-done | bytes 262160 | tf_op jit(solution)/shard_map/reduce_scatter | solution.py:42
  538.3 36.6 %reduce-scatter.9.cloned.1.call-done = bf16[128,1024]{1,0:T(8,128)(2,1)} async-done(((bf16[128,8192]{1,0:T(8,128)(2,1)}), bf16[128,1024]{1,0:T(8,128)(2,1)}) %reduce-scatter.9.cloned.1.call-update) | async-done | bytes 262160 | tf_op jit(solution)/shard_map/reduce_scatter | solution.py:42
  577.2 10.2 %all-to-all-start.7 = ((bf16[32,8,1024]{2,1,0:T(8,128)(2,1)}), bf16[32,8,1024]{2,1,0:T(8,128)(2,1)}, u32[]{:S(2)}, u32[]{:S(2)}) async-start(bf16[32,8,1024]{2,1,0:T(8,128)(2,1)} %copy.45), calls=%async_computation.11 | async-start | bytes 1048576 | tf_op jit(solution)/shard_map/all_to_all | solution.py:45
  592.5 9.1 %all-to-all-done.7 = bf16[32,8,1024]{2,1,0:T(8,128)(2,1)} async-done(((bf16[32,8,1024]{2,1,0:T(8,128)(2,1)}), bf16[32,8,1024]{2,1,0:T(8,128)(2,1)}, u32[]{:S(2)}, u32[]{:S(2)}) %all-to-all-start.7) | async-done | bytes 524320 | tf_op jit(solution)/shard_map/all_to_all | solution.py:45
  605.8 15.7 %psum.7 = f32[16,8]{1,0:T(8,128)S(1)} all-reduce(f32[16,8]{1,0:T(8,128)S(1)} %reduce_sum.95), channel_id=1, replica_groups=mesh['tp'=8,'ep'=32] {'tp'}, use_global_device_ids=true, to_apply=%region_16.21 | all-reduce | flops 128 | bytes 1024 | tf_op jit(solution)/shard_map/psum | solution.py:127
  (142 shorter events, 87.9 us)
Async XLA Ops:
  7.2 13.6 %copy-start = (bf16[56,8192]{1,0:T(8,128)(2,1)S(1)}, bf16[56,8192]{1,0:T(8,128)(2,1)}, u32[]{:S(2)}) copy-start(bf16[56,8192]{1,0:T(8,128)(2,1)} %param.21) | copy-start | bytes 2752516
  9.0 31.1 %all-to-all-start.1 = ((bf16[32,1,4]{2,1,0:T(2,128)(2,1)}), bf16[32,1,4]{2,1,0:T(2,128)(2,1)S(1)}, u32[]{:S(2)}, u32[]{:S(2)}) async-start(bf16[32,1,4]{2,1,0:T(2,128)(2,1)} %convert_element_type.135), calls=%async_computation.1 | async-start | bytes 32768 | tf_op jit(solution)/shard_map/all_to_all | solution.py:81
  20.7 3.2 copy-start.4
  23.9 3.2 copy-start.5
  40.0 58.7 %all-to-all-start.4 = ((bf16[32,4,8192]{2,1,0:T(4,128)(2,1)}), bf16[32,4,8192]{2,1,0:T(4,128)(2,1)}, u32[]{:S(2)}, u32[]{:S(2)}) async-start(bf16[32,4,8192]{2,1,0:T(4,128)(2,1)} %reshape.188), calls=%async_computation.4 | async-start | bytes 4194304 | tf_op jit(solution)/shard_map/all_to_all | solution.py:80
  98.7 56.0 %all-to-all-start.3 = ((bf16[32,4,8192]{2,1,0:T(4,128)(2,1)}), bf16[32,4,8192]{2,1,0:T(4,128)(2,1)}, u32[]{:S(2)}, u32[]{:S(2)}) async-start(bf16[32,4,8192]{2,1,0:T(4,128)(2,1)} %reshape.186), calls=%async_computation.3 | async-start | bytes 4194304 | tf_op jit(solution)/shard_map/all_to_all | solution.py:79
  107.7 52.5 %copy-start.22 = (f32[16,8]{0,1:T(8,128)S(1)}, f32[16,8]{0,1:T(8,128)}, u32[]{:S(2)}) copy-start(f32[16,8]{0,1:T(8,128)} %param.25) | copy-start | bytes 1540
  107.7 52.7 %copy-start.23 = (s32[16,8]{0,1:T(8,128)S(1)}, s32[16,8]{0,1:T(8,128)}, u32[]{:S(2)}) copy-start(s32[16,8]{0,1:T(8,128)} %param.24) | copy-start | bytes 1540
  107.7 53.2 %copy-start.2 = (bf16[16,8192]{1,0:T(8,128)(2,1)S(1)}, bf16[16,8192]{1,0:T(8,128)(2,1)}, u32[]{:S(2)}) copy-start(bf16[16,8192]{1,0:T(8,128)(2,1)} %param.18) | copy-start | bytes 786436
  154.7 53.0 %all-to-all-start.2 = ((bf16[32,4,8192]{2,1,0:T(4,128)(2,1)}), bf16[32,4,8192]{2,1,0:T(4,128)(2,1)S(1)}, u32[]{:S(2)}, u32[]{:S(2)}) async-start(bf16[32,4,8192]{2,1,0:T(4,128)(2,1)} %reshape.184), calls=%async_computation.2 | async-start | bytes 4194304 | tf_op jit(solution)/shard_map/all_to_all | solution.py:78
  161.0 5.2 copy-start.3
  207.7 99.2 %copy-start.17 = (bf16[32,4,8192]{2,1,0:T(4,128)(2,1)}, bf16[32,4,8192]{2,1,0:T(4,128)(2,1)S(1)}, u32[]{:S(2)}) copy-start(bf16[32,4,8192]{2,1,0:T(4,128)(2,1)S(1)} %all-to-all-done.2) | copy-start | bytes 6291460
  306.9 98.2 %all-to-all-start.6 = ((bf16[32,8,8192]{2,1,0:T(8,128)(2,1)}), bf16[32,8,8192]{2,1,0:T(8,128)(2,1)}, u32[]{:S(2)}, u32[]{:S(2)}) async-start(bf16[32,8,8192]{2,1,0:T(8,128)(2,1)} %get-tuple-element.50), calls=%async_computation.8 | async-start | bytes 8388608 | tf_op jit(solution)/shard_map/all_to_all | solution.py:36
  312.5 147.4 %reduce-scatter.7.cloned.1.call-start = ((), (), s32[]{:S(2)}) async-start(), calls=%async_computation.13 | async-start | bytes 2359296 | tf_op jit(solution)/shard_map/reduce_scatter | solution.py:42
  351.4 3.8 copy-start.6
  351.4 2.9 copy-start.8
  417.7 4.1 copy-start.12
  426.4 72.0 %reduce-scatter.5.cloned.1.call-start = ((), (), s32[]{:S(2)}) async-start(), calls=%async_computation.12 | async-start | bytes 2359296 | tf_op jit(solution)/shard_map/reduce_scatter | solution.py:42
  432.9 2.3 copy-start.9
  432.9 3.1 copy-start.15
  439.8 97.4 %reduce-scatter.11.cloned.1.call-start = ((), (), s32[]{:S(2)}) async-start(), calls=%async_computation.15 | async-start | bytes 2359296 | tf_op jit(solution)/shard_map/reduce_scatter | solution.py:42
  440.1 2.1 copy-start.10
  444.3 130.6 %reduce-scatter.9.cloned.1.call-start = ((), (), s32[]{:S(2)}) async-start(), calls=%async_computation.14 | async-start | bytes 2359296 | tf_op jit(solution)/shard_map/reduce_scatter | solution.py:42
  444.4 2.1 copy-start.11
  452.3 2.0 copy-start.7
  454.3 2.0 copy-start.14
  456.3 2.0 copy-start.16
  500.7 76.6 %all-to-all-start.5 = ((bf16[32,8,1024]{2,1,0:T(8,128)(2,1)}), bf16[32,8,1024]{2,1,0:T(8,128)(2,1)S(1)}, u32[]{:S(2)}, u32[]{:S(2)}) async-start(bf16[32,8,1024]{2,1,0:T(8,128)(2,1)} %copy.42), calls=%async_computation.7 | async-start | bytes 1048576 | tf_op jit(solution)/shard_map/all_to_all | solution.py:45
  577.2 24.3 %all-to-all-start.7 = ((bf16[32,8,1024]{2,1,0:T(8,128)(2,1)}), bf16[32,8,1024]{2,1,0:T(8,128)(2,1)}, u32[]{:S(2)}, u32[]{:S(2)}) async-start(bf16[32,8,1024]{2,1,0:T(8,128)(2,1)} %copy.45), calls=%async_computation.11 | async-start | bytes 1048576 | tf_op jit(solution)/shard_map/all_to_all | solution.py:45
  587.4 1.8 copy-start.20
  591.7 13.8 %copy-start.21 = (f32[16,1024]{1,0:T(8,128)S(1)}, f32[16,1024]{1,0:T(8,128)}, u32[]{:S(2)}) copy-start(f32[16,1024]{1,0:T(8,128)} %dynamic-slice_convert_fusion) | copy-start | bytes 196612
  591.7 30.5 %copy-start.1 = (bf16[56,8192]{1,0:T(8,128)(2,1)S(1)}, bf16[56,8192]{1,0:T(8,128)(2,1)}, u32[]{:S(2)}) copy-start(bf16[56,8192]{1,0:T(8,128)(2,1)} %param.21) | copy-start | bytes 2752516
  (3 other events, 4.5 us)
Sparse Core Ops, SparseCore 0:
  426.5 33.3 reduce-scatter.6
  463.0 35.3 reduce-scatter.4
  501.5 35.6 reduce-scatter.10
  539.6 35.2 reduce-scatter.8
where the time goes:
time: 631 us; the launch traced here: 629 us
  waiting for transfers between devices  276 us (44%)
  blocking collectives  115 us (18%)
  local copies, waits for them, and re-layouts  103 us (16%)
  starting transfers between devices  60.4 us (10%)
  matrix products  31.7 us (5%)
  other arithmetic  27.9 us (4%)
  between operations  14.3 us (2%)
    all_to_all x1, blocking collectives, dispatch(): return lax.all_to_all(rows, 'ep', split_axis=0, concat_axis=0, tiled=True)  99.2 us
    reduce_scatter x4, waiting for transfers between devices, to_sources(): lax.psum_scatter(term.astype(jnp.bfloat16), 'tp', scatter_dimension=1, ti...  97.3 us
    all_to_all x1, waiting for transfers between devices, dispatch(): return lax.all_to_all(rows, 'ep', split_axis=0, concat_axis=0, tiled=True)  49.9 us
    all_to_all x1, waiting for transfers between devices, body(): lax.all_to_all(pack(w_up), 'ep', split_axis=0, concat_axis=0, tiled=True)  47 us
    all_to_all x1, waiting for transfers between devices, body(): lax.all_to_all(pack(w_down), 'ep', split_axis=0, concat_axis=0, tiled=True)  44.7 us
    all_to_all x1, waiting for transfers between devices, body(): lax.all_to_all(pack(w_gate), 'ep', split_axis=0, concat_axis=0, tiled=True)  28.3 us
    gather x7, local copies, waits for them, and re-layouts, pick_rows(): taken = jnp.take(rows, index, axis=0)  24.2 us
    all_to_all x2, starting transfers between devices, to_sources(): lax.all_to_all(stacked, 'ep', split_axis=0, concat_axis=0, tiled=True)  20.3 us
  transfers between devices with their start and end apart: 11, of which 9 were waited for; matrix products, arithmetic and copies ran while one was open for 21% of the time, Pallas kernels for 0%

commit v1 on v0

--- a/solution.py
+++ b/solution.py
@@ -6,6 +6,11 @@
 NL = 56
 E_DEV = 2
 TOPK = 8
+
+
+def face_detail(named_axis, xs):
+    even = lax.all_gather(xs, named_axis).sum(axis=0)
+    return even
 
 
 def earlier_same(labels):
@@ -124,7 +129,7 @@
     partial_value = jnp.sum(
         per_choice.reshape(tok_dev, TOPK, local_width) * cot_local[:, None, :], 2
     )
-    d_weight = lax.psum(partial_value, "tp")
+    d_weight = face_detail("tp", partial_value)
     slot_weight = jnp.take(choice_weight.reshape(-1), choice_of_slot, axis=0)
     slot_cot = jnp.take(cotangent, choice_of_slot // TOPK, axis=0).astype(jnp.float32)
     scaled_rows = (slot_weight[:, None] * slot_cot).astype(jnp.bfloat16)

time: 631 us -> 636 us (level); the launches traced: 629 us -> 626 us
    psum x1 -> x0, blocking collectives: 15.7 us -> none  [body(): d_weight = lax.psum(partial_value, 'tp')]
    all_gather x0 -> x1, blocking collectives: none -> 13.1 us  [face_detail(): even = lax.all_gather(xs, named_axis).sum(axis=0)]
where the time goes in v1:
time: 636 us; the launch traced here: 626 us
  waiting for transfers between devices  276 us (43%)
  blocking collectives  112 us (18%)
  local copies, waits for them, and re-layouts  103 us (16%)
  starting transfers between devices  60.8 us (10%)
  matrix products  31.7 us (5%)
  other arithmetic  28.5 us (4%)
  between operations  14.5 us (2%)
    all_to_all x1, blocking collectives, dispatch(): return lax.all_to_all(rows, 'ep', split_axis=0, concat_axis=0, tiled=True)  99.2 us
    reduce_scatter x4, waiting for transfers between devices, to_sources(): lax.psum_scatter(term.astype(jnp.bfloat16), 'tp', scatter_dimension=1, ti...  97.1 us
    all_to_all x1, waiting for transfers between devices, dispatch(): return lax.all_to_all(rows, 'ep', split_axis=0, concat_axis=0, tiled=True)  50 us
    all_to_all x1, waiting for transfers between devices, body(): lax.all_to_all(pack(w_up), 'ep', split_axis=0, concat_axis=0, tiled=True)  47 us
    all_to_all x1, waiting for transfers between devices, body(): lax.all_to_all(pack(w_down), 'ep', split_axis=0, concat_axis=0, tiled=True)  44.7 us
    all_to_all x1, waiting for transfers between devices, body(): lax.all_to_all(pack(w_gate), 'ep', split_axis=0, concat_axis=0, tiled=True)  28.2 us
    gather x7, local copies, waits for them, and re-layouts, pick_rows(): taken = jnp.take(rows, index, axis=0)  24.2 us
    all_to_all x2, starting transfers between devices, to_sources(): lax.all_to_all(stacked, 'ep', split_axis=0, concat_axis=0, tiled=True)  20.2 us
  transfers between devices with their start and end apart: 11, of which 9 were waited for; matrix products, arithmetic and copies ran while one was open for 21% of the time, Pallas kernels for 0%

profile of v1, /device:TPU:2, one launch (start us, length us, event | category | flops | bytes accessed | tf_op | source)
XLA Modules:
  0.0 626.5 jit_solution(1794479664540960971)
XLA Ops:
  9.0 11.6 %all-to-all-start.1 = ((bf16[32,1,4]{2,1,0:T(2,128)(2,1)}), bf16[32,1,4]{2,1,0:T(2,128)(2,1)S(1)}, u32[]{:S(2)}, u32[]{:S(2)}) async-start(bf16[32,1,4]{2,1,0:T(2,128)(2,1)} %convert_element_type.135), calls=%async_computation.1 | async-start | bytes 32768 | tf_op jit(solution)/shard_map/all_to_all | solution.py:86
  30.3 5.6 select_select_fusion.2
  35.9 4.1 reshape.189
  40.0 9.8 %all-to-all-start.4 = ((bf16[32,4,8192]{2,1,0:T(4,128)(2,1)}), bf16[32,4,8192]{2,1,0:T(4,128)(2,1)}, u32[]{:S(2)}, u32[]{:S(2)}) async-start(bf16[32,4,8192]{2,1,0:T(4,128)(2,1)} %reshape.189), calls=%async_computation.4 | async-start | bytes 4194304 | tf_op jit(solution)/shard_map/all_to_all | solution.py:85
  49.9 4.1 reshape.187
  54.0 44.7 %all-to-all-done.4 = bf16[32,4,8192]{2,1,0:T(4,128)(2,1)} async-done(((bf16[32,4,8192]{2,1,0:T(4,128)(2,1)}), bf16[32,4,8192]{2,1,0:T(4,128)(2,1)}, u32[]{:S(2)}, u32[]{:S(2)}) %all-to-all-start.4) | async-done | bytes 2097184 | tf_op jit(solution)/shard_map/all_to_all | solution.py:85
  98.7 6.8 %all-to-all-start.3 = ((bf16[32,4,8192]{2,1,0:T(4,128)(2,1)}), bf16[32,4,8192]{2,1,0:T(4,128)(2,1)}, u32[]{:S(2)}, u32[]{:S(2)}) async-start(bf16[32,4,8192]{2,1,0:T(4,128)(2,1)} %reshape.187), calls=%async_computation.3 | async-start | bytes 4194304 | tf_op jit(solution)/shard_map/all_to_all | solution.py:84
  107.7 47.0 %all-to-all-done.3 = bf16[32,4,8192]{2,1,0:T(4,128)(2,1)} async-done(((bf16[32,4,8192]{2,1,0:T(4,128)(2,1)}), bf16[32,4,8192]{2,1,0:T(4,128)(2,1)}, u32[]{:S(2)}, u32[]{:S(2)}) %all-to-all-start.3) | async-done | bytes 2097184 | tf_op jit(solution)/shard_map/all_to_all | solution.py:84
  154.7 6.1 all-to-all-start.2
  161.6 5.2 gather_fusion.9
  166.7 5.1 gather_fusion.1
  173.9 6.2 fusion.9
  180.0 28.2 %all-to-all-done.2 = bf16[32,4,8192]{2,1,0:T(4,128)(2,1)S(1)} async-done(((bf16[32,4,8192]{2,1,0:T(4,128)(2,1)}), bf16[32,4,8192]{2,1,0:T(4,128)(2,1)S(1)}, u32[]{:S(2)}, u32[]{:S(2)}) %all-to-all-start.2) | async-done | bytes 2097184 | tf_op jit(solution)/shard_map/all_to_all | solution.py:83
  208.2 99.2 %all_to_all.41 = bf16[32,8,8192]{2,1,0:T(8,128)(2,1)} all-to-all(bf16[32,8,8192]{2,1,0:T(8,128)(2,1)} %get-tuple-element.39), channel_id=1, replica_groups=mesh['tp'=8,'ep'=32] {'ep'}, dimensions={0} | all-to-all | bytes 8388608 | tf_op jit(solution)/shard_map/all_to_all | solution.py:41
  307.4 5.6 all-to-all-start.6
  327.7 3.2 gather_fusion.3
  330.8 5.9 select_select_fusion.1
  336.7 7.2 %reshape.184 = bf16[32,2,4,8192]{3,2,1,0:T(4,128)(2,1)} reshape(bf16[32,8,8192]{2,1,0:T(8,128)(2,1)} %all_to_all.41) | data formatting | bytes 8388608 | tf_op jit(solution)/shard_map/reshape | solution.py:110
  343.9 5.4 fusion.45
  355.6 50.0 %all-to-all-done.6 = bf16[32,8,8192]{2,1,0:T(8,128)(2,1)} async-done(((bf16[32,8,8192]{2,1,0:T(8,128)(2,1)}), bf16[32,8,8192]{2,1,0:T(8,128)(2,1)}, u32[]{:S(2)}, u32[]{:S(2)}) %all-to-all-start.6) | async-done | bytes 4194336 | tf_op jit(solution)/shard_map/all_to_all | solution.py:41
  405.6 7.2 %reshape.195 = bf16[32,2,4,8192]{3,2,1,0:T(4,128)(2,1)} reshape(bf16[32,8,8192]{2,1,0:T(8,128)(2,1)} %all-to-all-done.6) | data formatting | bytes 8388608 | tf_op jit(solution)/shard_map/reshape | solution.py:138
  412.8 5.4 fusion.44
  418.2 4.1 reshape_squeeze.15
  429.4 3.9 reshape_squeeze.14
  461.5 37.2 %reduce-scatter.5.cloned.1.call-done = bf16[128,1024]{1,0:T(8,128)(2,1)} async-done(((bf16[128,8192]{1,0:T(8,128)(2,1)}), bf16[128,1024]{1,0:T(8,128)(2,1)}) %reduce-scatter.5.cloned.1.call-update) | async-done | bytes 262160 | tf_op jit(solution)/shard_map/reduce_scatter | solution.py:47
  501.0 10.1 %all-to-all-start.5 = ((bf16[32,8,1024]{2,1,0:T(8,128)(2,1)}), bf16[32,8,1024]{2,1,0:T(8,128)(2,1)S(1)}, u32[]{:S(2)}, u32[]{:S(2)}) async-start(bf16[32,8,1024]{2,1,0:T(8,128)(2,1)} %copy.42), calls=%async_computation.7 | async-start | bytes 1048576 | tf_op jit(solution)/shard_map/all_to_all | solution.py:50
  511.1 3.2 pad_maximum_fusion.2
  514.3 23.2 %reduce-scatter.11.cloned.1.call-done = bf16[128,1024]{1,0:T(8,128)(2,1)} async-done(((bf16[128,8192]{1,0:T(8,128)(2,1)}), bf16[128,1024]{1,0:T(8,128)(2,1)}) %reduce-scatter.11.cloned.1.call-update) | async-done | bytes 262160 | tf_op jit(solution)/shard_map/reduce_scatter | solution.py:47
  538.6 36.5 %reduce-scatter.9.cloned.1.call-done = bf16[128,1024]{1,0:T(8,128)(2,1)} async-done(((bf16[128,8192]{1,0:T(8,128)(2,1)}), bf16[128,1024]{1,0:T(8,128)(2,1)}) %reduce-scatter.9.cloned.1.call-update) | async-done | bytes 262160 | tf_op jit(solution)/shard_map/reduce_scatter | solution.py:47
  577.4 10.1 %all-to-all-start.7 = ((bf16[32,8,1024]{2,1,0:T(8,128)(2,1)}), bf16[32,8,1024]{2,1,0:T(8,128)(2,1)}, u32[]{:S(2)}, u32[]{:S(2)}) async-start(bf16[32,8,1024]{2,1,0:T(8,128)(2,1)} %copy.45), calls=%async_computation.11 | async-start | bytes 1048576 | tf_op jit(solution)/shard_map/all_to_all | solution.py:50
  592.7 9.0 %all-to-all-done.7 = bf16[32,8,1024]{2,1,0:T(8,128)(2,1)} async-done(((bf16[32,8,1024]{2,1,0:T(8,128)(2,1)}), bf16[32,8,1024]{2,1,0:T(8,128)(2,1)}, u32[]{:S(2)}, u32[]{:S(2)}) %all-to-all-start.7) | async-done | bytes 524320 | tf_op jit(solution)/shard_map/all_to_all | solution.py:50
  605.9 13.1 %all_gather.7 = f32[8,16,8]{1,2,0:T(8,128)S(1)} all-gather(f32[1,16,8]{1,2,0:T(8,128)S(1)} %copy.46), channel_id=1, replica_groups=mesh['tp'=8,'ep'=32] {'tp'}, dimensions={0}, use_global_device_ids=true | all-gather | bytes 4608 | tf_op jit(solution)/shard_map/all_gather | solution.py:12
  (143 shorter events, 87.9 us)
Async XLA Ops:
  7.2 13.6 %copy-start = (bf16[56,8192]{1,0:T(8,128)(2,1)S(1)}, bf16[56,8192]{1,0:T(8,128)(2,1)}, u32[]{:S(2)}) copy-start(bf16[56,8192]{1,0:T(8,128)(2,1)} %param.21) | copy-start | bytes 2752516
  9.0 31.1 %all-to-all-start.1 = ((bf16[32,1,4]{2,1,0:T(2,128)(2,1)}), bf16[32,1,4]{2,1,0:T(2,128)(2,1)S(1)}, u32[]{:S(2)}, u32[]{:S(2)}) async-start(bf16[32,1,4]{2,1,0:T(2,128)(2,1)} %convert_element_type.135), calls=%async_computation.1 | async-start | bytes 32768 | tf_op jit(solution)/shard_map/all_to_all | solution.py:86
  20.7 3.2 copy-start.4
  23.9 3.2 copy-start.5
  40.0 58.7 %all-to-all-start.4 = ((bf16[32,4,8192]{2,1,0:T(4,128)(2,1)}), bf16[32,4,8192]{2,1,0:T(4,128)(2,1)}, u32[]{:S(2)}, u32[]{:S(2)}) async-start(bf16[32,4,8192]{2,1,0:T(4,128)(2,1)} %reshape.189), calls=%async_computation.4 | async-start | bytes 4194304 | tf_op jit(solution)/shard_map/all_to_all | solution.py:85
  98.7 56.0 %all-to-all-start.3 = ((bf16[32,4,8192]{2,1,0:T(4,128)(2,1)}), bf16[32,4,8192]{2,1,0:T(4,128)(2,1)}, u32[]{:S(2)}, u32[]{:S(2)}) async-start(bf16[32,4,8192]{2,1,0:T(4,128)(2,1)} %reshape.187), calls=%async_computation.3 | async-start | bytes 4194304 | tf_op jit(solution)/shard_map/all_to_all | solution.py:84
  107.7 53.1 %copy-start.22 = (f32[16,8]{0,1:T(8,128)S(1)}, f32[16,8]{0,1:T(8,128)}, u32[]{:S(2)}) copy-start(f32[16,8]{0,1:T(8,128)} %param.25) | copy-start | bytes 1540
  107.7 53.3 %copy-start.23 = (s32[16,8]{0,1:T(8,128)S(1)}, s32[16,8]{0,1:T(8,128)}, u32[]{:S(2)}) copy-start(s32[16,8]{0,1:T(8,128)} %param.24) | copy-start | bytes 1540
  107.7 53.8 %copy-start.2 = (bf16[16,8192]{1,0:T(8,128)(2,1)S(1)}, bf16[16,8192]{1,0:T(8,128)(2,1)}, u32[]{:S(2)}) copy-start(bf16[16,8192]{1,0:T(8,128)(2,1)} %param.18) | copy-start | bytes 786436
  154.7 53.5 %all-to-all-start.2 = ((bf16[32,4,8192]{2,1,0:T(4,128)(2,1)}), bf16[32,4,8192]{2,1,0:T(4,128)(2,1)S(1)}, u32[]{:S(2)}, u32[]{:S(2)}) async-start(bf16[32,4,8192]{2,1,0:T(4,128)(2,1)} %reshape.185), calls=%async_computation.2 | async-start | bytes 4194304 | tf_op jit(solution)/shard_map/all_to_all | solution.py:83
  161.6 5.2 copy-start.3
  208.2 99.2 %copy-start.17 = (bf16[32,4,8192]{2,1,0:T(4,128)(2,1)}, bf16[32,4,8192]{2,1,0:T(4,128)(2,1)S(1)}, u32[]{:S(2)}) copy-start(bf16[32,4,8192]{2,1,0:T(4,128)(2,1)S(1)} %all-to-all-done.2) | copy-start | bytes 6291460
  307.4 98.2 %all-to-all-start.6 = ((bf16[32,8,8192]{2,1,0:T(8,128)(2,1)}), bf16[32,8,8192]{2,1,0:T(8,128)(2,1)}, u32[]{:S(2)}, u32[]{:S(2)}) async-start(bf16[32,8,8192]{2,1,0:T(8,128)(2,1)} %get-tuple-element.38), calls=%async_computation.8 | async-start | bytes 8388608 | tf_op jit(solution)/shard_map/all_to_all | solution.py:41
  313.0 147.4 %reduce-scatter.7.cloned.1.call-start = ((), (), s32[]{:S(2)}) async-start(), calls=%async_computation.13 | async-start | bytes 2359296 | tf_op jit(solution)/shard_map/reduce_scatter | solution.py:47
  351.8 3.8 copy-start.6
  351.8 2.9 copy-start.8
  418.2 4.1 copy-start.12
  426.8 71.9 %reduce-scatter.5.cloned.1.call-start = ((), (), s32[]{:S(2)}) async-start(), calls=%async_computation.12 | async-start | bytes 2359296 | tf_op jit(solution)/shard_map/reduce_scatter | solution.py:47
  433.4 2.3 copy-start.9
  433.4 3.1 copy-start.15
  440.3 97.2 %reduce-scatter.11.cloned.1.call-start = ((), (), s32[]{:S(2)}) async-start(), calls=%async_computation.15 | async-start | bytes 2359296 | tf_op jit(solution)/shard_map/reduce_scatter | solution.py:47
  440.5 2.1 copy-start.10
  444.7 130.4 %reduce-scatter.9.cloned.1.call-start = ((), (), s32[]{:S(2)}) async-start(), calls=%async_computation.14 | async-start | bytes 2359296 | tf_op jit(solution)/shard_map/reduce_scatter | solution.py:47
  444.8 2.1 copy-start.11
  452.7 2.0 copy-start.7
  454.7 2.0 copy-start.14
  456.7 2.0 copy-start.16
  501.0 76.4 %all-to-all-start.5 = ((bf16[32,8,1024]{2,1,0:T(8,128)(2,1)}), bf16[32,8,1024]{2,1,0:T(8,128)(2,1)S(1)}, u32[]{:S(2)}, u32[]{:S(2)}) async-start(bf16[32,8,1024]{2,1,0:T(8,128)(2,1)} %copy.42), calls=%async_computation.7 | async-start | bytes 1048576 | tf_op jit(solution)/shard_map/all_to_all | solution.py:50
  577.4 24.3 %all-to-all-start.7 = ((bf16[32,8,1024]{2,1,0:T(8,128)(2,1)}), bf16[32,8,1024]{2,1,0:T(8,128)(2,1)}, u32[]{:S(2)}, u32[]{:S(2)}) async-start(bf16[32,8,1024]{2,1,0:T(8,128)(2,1)} %copy.45), calls=%async_computation.11 | async-start | bytes 1048576 | tf_op jit(solution)/shard_map/all_to_all | solution.py:50
  587.6 1.8 copy-start.20
  591.8 13.8 %copy-start.21 = (f32[16,1024]{1,0:T(8,128)S(1)}, f32[16,1024]{1,0:T(8,128)}, u32[]{:S(2)}) copy-start(f32[16,1024]{1,0:T(8,128)} %dynamic-slice_convert_fusion) | copy-start | bytes 196612
  591.8 27.9 %copy-start.1 = (bf16[56,8192]{1,0:T(8,128)(2,1)S(1)}, bf16[56,8192]{1,0:T(8,128)(2,1)}, u32[]{:S(2)}) copy-start(bf16[56,8192]{1,0:T(8,128)(2,1)} %param.21) | copy-start | bytes 2752516
  (3 other events, 4.5 us)
Sparse Core Ops, SparseCore 0:
  426.9 33.3 reduce-scatter.6
  463.5 35.2 reduce-scatter.4
  501.9 35.5 reduce-scatter.10
  539.9 35.2 reduce-scatter.8
